TPU v7x, 256 devices: a whole 4x4x8 slice. The times are simulated.
256 devices in a mesh: row: 8 (over z), col: 32 (over x, y, core).
Axes of the slice: x: 4, y: 4, z: 8, core: 2. Of those that a mesh axis runs over, the one named last changes fastest.
Arguments:
- tile_data: bfloat16 [8, 32, 32, 256, 256], P('row', 'col'), may hold values from -0.125 to 0.125
- tile_row_block: int32 [8, 32, 32], P('row', 'col'), may hold values from 0 to 63
- tile_column_block: int32 [8, 32, 32], P('row', 'col'), may hold values from 0 to 63
- tile_count: int32 [8, 32], P('row', 'col'), may hold values from 1 to 32, as said below
- saved_primal: float32 [3, 524288], P(None, 'col'), may hold values from 0 to 1
- saved_dual: float32 [3, 131072], P(None, 'row'), may hold values from 0 to 1
- primal_mask: int32 [3, 524288], P(None, 'col'), may hold values 0 or 1
- dual_mask: int32 [3, 131072], P(None, 'row'), may hold values 0 or 1
- cost_vector: float32 [524288], P('col'), may hold values from -6 to 6
- demand: float32 [131072], P('row'), may hold values from -6 to 6
- upper_bound: float32 [524288], P('col'), may hold values from 0.5 to 1.5
- step_sizes: float32 [2], replicated, may hold values from 0.2 to 0.4
- primal_cotangent: float32 [524288], P('col'), may hold values from -6 to 6
- dual_cotangent: float32 [131072], P('row'), may hold values from -6 to 6
Outputs:
- primal_adjoint: float32 [524288], P('col')
- dual_adjoint: float32 [131072], P(('row', 'col'))
- step_gradients: float32 [2], replicated
Inputs may be any that keep to these rules, and one draw needn't show every extreme that they name: `tile_count`: block positions may repeat, and tiles at one position add; slots at and beyond a device's count are ignored. In every index of row some device has 32 live slots.
All inputs are finite; a program needn't handle non-finite values. No bound on the sum of `primal_mask` or of `dual_mask` on one device may be relied on, other than what follows from the above.
Results may differ from a plain program's by a relative error of at most 0.00071.
Values may be sent and summed in bfloat16 or wider, within the bound.
A program may use at most 64 MiB of HBM per device.

v0:
```python
import math
import jax
import jax.numpy as jnp
from jax import lax
from jax.sharding import PartitionSpec as P


def block_terms(tile_part, in_part, out_part, live_part, vectors, out_blocks, transpose):
    tile_width = tile_part.shape[-1]
    blocks = vectors.reshape(vectors.shape[0], -1, tile_width)
    picked = jnp.take(blocks, in_part, axis=1)
    einsum_form = "sij,bsi->bsj" if transpose else "sij,bsj->bsi"
    products = jnp.einsum(einsum_form, tile_part, picked, preferred_element_type=jnp.float32)
    products = products * live_part[None, :, None]
    selector = (out_part[:, None] == jnp.arange(out_blocks, dtype=jnp.int32)[None, :]).astype(
        jnp.float32
    )
    summed = jnp.einsum("sn,bsi->bni", selector, products, precision=lax.Precision.HIGHEST)
    return summed.reshape(vectors.shape[0], out_blocks * tile_width)


def tile_apply(tile_stack, in_index, out_index, live_count, vectors, out_blocks, transpose):
    slot_count = tile_stack.shape[0]
    live_slots = (jnp.arange(slot_count, dtype=jnp.int32) < live_count).astype(jnp.float32)
    return block_terms(tile_stack, in_index, out_index, live_slots, vectors, out_blocks, transpose)


def local(
    tile_data,
    tile_row_block,
    tile_column_block,
    tile_count,
    saved_primal,
    saved_dual,
    primal_mask,
    dual_mask,
    cost_vector,
    demand,
    upper_bound,
    step_sizes,
    primal_cotangent,
    dual_cotangent,
):
    slot_count = tile_data.shape[2]
    tile_width = tile_data.shape[-1]
    tile_stack = tile_data.reshape(slot_count, tile_width, tile_width)
    row_blocks = tile_row_block.reshape(slot_count)
    column_blocks = tile_column_block.reshape(slot_count)
    live_count = tile_count.reshape(())
    iterations = saved_primal.shape[0]
    row_length = saved_dual.shape[1]
    column_length = saved_primal.shape[1]
    share_rows = row_length // lax.axis_size("col")
    share_start = lax.axis_index("col") * share_rows
    column_part = column_length // lax.axis_size("row")
    column_start = lax.axis_index("row") * column_part
    tau = step_sizes[0]
    sigma = step_sizes[1]

    def forward(vectors):
        return tile_apply(
            tile_stack,
            column_blocks,
            row_blocks,
            live_count,
            vectors,
            row_length // tile_width,
            False,
        )

    def backward(vectors):
        return tile_apply(
            tile_stack,
            row_blocks,
            column_blocks,
            live_count,
            vectors,
            column_length // tile_width,
            True,
        )

    def row_share(array):
        return lax.dynamic_slice_in_dim(array, share_start, share_rows, array.ndim - 1)

    def column_share(array):
        return lax.dynamic_slice_in_dim(array, column_start, column_part, array.ndim - 1)

    dual_partial = backward(saved_dual.astype(jnp.bfloat16))
    reduced = cost_vector[None, :] - lax.psum(dual_partial, "row")
    half = jnp.clip(saved_primal - tau * reduced, 0.0, upper_bound[None, :])
    extrapolated = (2.0 * half - saved_primal).astype(jnp.bfloat16)
    masks_x = primal_mask.astype(jnp.float32)
    adjoint_x = primal_cotangent
    partial_value = forward(extrapolated)
    residual_share = row_share(demand[None, :] - lax.psum(partial_value, "col"))
    adjoint_y = dual_cotangent
    masks_y = dual_mask.astype(jnp.float32)
    anchor_x = jnp.zeros_like(adjoint_x)
    anchor_y = jnp.zeros_like(adjoint_y)
    tau_sum = jnp.zeros((), jnp.float32)
    sigma_sum = jnp.zeros((), jnp.float32)
    for step in reversed(range(iterations)):
        weight = (step + 1.0) / (step + 2.0)
        anchor_x = anchor_x + (1.0 - weight) * adjoint_x
        anchor_y = anchor_y + (1.0 - weight) * adjoint_y
        dual_term = masks_y[step] * weight * adjoint_y
        sigma_local = jnp.sum(row_share(dual_term) * residual_share[step])
        spread = dual_term.astype(jnp.bfloat16)
        back_partial = backward(spread[None, :])
        back = lax.psum(back_partial, "row")[0]
        primal_term = masks_x[step] * (weight * adjoint_x - 2.0 * sigma * back)
        tau_local = jnp.sum(-column_share(primal_term) * column_share(reduced[step]))
        primal_input = primal_term.astype(jnp.bfloat16)
        adjoint_x = primal_term + sigma * back
        image = forward(primal_input[None, :])
        image_rows = lax.psum(image, "col")[0]
        adjoint_y = dual_term + tau * image_rows
        tau_total, sigma_total = lax.psum((tau_local, sigma_local), ("row", "col"))
        tau_sum = tau_sum + tau_total
        sigma_sum = sigma_sum + sigma_total
    primal_adjoint = adjoint_x + anchor_x
    dual_adjoint = row_share(adjoint_y + anchor_y)
    total_columns = column_length * lax.axis_size("col")
    total_rows = row_length * lax.axis_size("row")
    gradients = jnp.stack([tau_sum / math.sqrt(total_columns), sigma_sum / math.sqrt(total_rows)])
    return (primal_adjoint, dual_adjoint, gradients)


def solution(mesh):
    placed = (
        P("row", "col", None, None, None),
        P("row", "col", None),
        P("row", "col", None),
        P("row", "col"),
        P(None, "col"),
        P(None, "row"),
        P(None, "col"),
        P(None, "row"),
        P("col"),
        P("row"),
        P("col"),
        P(),
        P("col"),
        P("row"),
    )
    return jax.shard_map(
        local,
        mesh=mesh,
        in_specs=placed,
        out_specs=(P("col"), P(("row", "col")), P()),
        check_vma=False,
    )
```

profile of v0, /device:TPU:1, one launch (start us, length us, event | category | flops | bytes accessed | tf_op | source)
XLA Modules:
  0.0 686.6 jit_solution(12237295428847181642)
XLA Ops:
  8.7 1.0 convert_element_type.25
  12.1 2.8 fusion.14
  17.5 68.9 %all-reduce.10.cloned.1.call-done = f32[1,16384]{1,0:T(1,128)} async-done(((f32[1,16384]{1,0:T(1,128)}), f32[1,16384]{1,0:T(1,128)}) %all-reduce.10.cloned.1.call-update) | async-done | bytes 65552 | tf_op jit(solution)/shard_map/psum | solution.py:110
  86.4 1.6 broadcast_multiply_fusion.5
  88.7 3.4 fusion.12
  93.9 108.8 %all-reduce.12.cloned.1.call-done = f32[1,16384]{1,0:T(1,128)} async-done(((f32[1,16384]{1,0:T(1,128)}), f32[1,16384]{1,0:T(1,128)}) %all-reduce.12.cloned.1.call-update) | async-done | bytes 65552 | tf_op jit(solution)/shard_map/psum | solution.py:116
  202.7 1.5 broadcast_multiply_fusion.2
  204.9 2.8 fusion.10
  208.9 2.9 fusion.2
  211.7 62.4 %all-reduce.14.cloned.1.call-done = f32[1,16384]{1,0:T(1,128)} async-done(((f32[1,16384]{1,0:T(1,128)}), f32[1,16384]{1,0:T(1,128)}) %all-reduce.14.cloned.1.call-update) | async-done | bytes 65552 | tf_op jit(solution)/shard_map/psum | solution.py:110
  274.1 1.6 broadcast_multiply_fusion.4
  276.4 3.4 fusion.8
  282.1 108.3 %all-reduce.16.cloned.1.call-done = f32[1,16384]{1,0:T(1,128)} async-done(((f32[1,16384]{1,0:T(1,128)}), f32[1,16384]{1,0:T(1,128)}) %all-reduce.16.cloned.1.call-update) | async-done | bytes 65552 | tf_op jit(solution)/shard_map/psum | solution.py:116
  390.4 1.5 broadcast_multiply_fusion.1
  392.7 2.8 fusion.6
  397.3 66.3 %all-reduce.20.cloned.1.call-done = (f32[1,16384]{1,0:T(1,128)}, f32[3,16384]{1,0:T(4,128)}) async-done(((f32[1,16384]{1,0:T(1,128)}, f32[3,16384]{1,0:T(4,128)}), (f32[1,16384]{1,0:T(1,128)}, f32[3,16384]{1,0:T(4,128)})) %all-reduce.20.cloned.1.call-update) | async-done | bytes 262160 | tf_op jit(solution)/shard_map/psum | solution.py:110
  463.7 1.8 subtract_convert_fusion
  465.6 1.6 broadcast_multiply_fusion.3
  467.8 3.4 fusion
  473.8 3.4 fusion.4
  481.4 112.0 %all-reduce.18.cloned.1.call-done = (f32[1,16384]{1,0:T(1,128)}, f32[3,16384]{1,0:T(4,128)}) async-done(((f32[1,16384]{1,0:T(1,128)}, f32[3,16384]{1,0:T(4,128)}), (f32[1,16384]{1,0:T(1,128)}, f32[3,16384]{1,0:T(4,128)})) %all-reduce.18.cloned.1.call-update) | async-done | bytes 262160 | tf_op jit(solution)/shard_map/psum | solution.py:116
  595.5 1.5 broadcast_multiply_fusion
  598.3 1.9 multiply_reduce_fusion.3
  601.6 76.4 %all-reduce = (f32[]{:T(128)}, f32[]{:T(128)}) all-reduce(f32[]{:T(128)S(6)} %add.120, f32[]{:T(128)S(6)} %add.118), channel_id=1, replica_groups=mesh['row'=8,'col'=32] {'row','col'}, use_global_device_ids=true, to_apply=%region_15.18 | all-reduce | flops 2 | bytes 16 | tf_op jit(solution)/shard_map/psum | solution.py:118
  (96 shorter events, 23.9 us)
Async XLA Ops:
  7.2 7.8 %copy-start.6 = (s32[1,1,32]{2,1,0:T(1,128)S(1)}, s32[1,1,32]{2,1,0:T(1,128)}, u32[]{:S(2)}) copy-start(s32[1,1,32]{2,1,0:T(1,128)} %param.20) | copy-start | bytes 388
  7.2 8.9 %copy-start.8 = (f32[2]{0:T(128)S(1)}, f32[2]{0:T(128)}, u32[]{:S(2)}) copy-start(f32[2]{0:T(128)} %param.29) | copy-start | bytes 28
  7.2 9.4 %copy-start.1 = (s32[3,16384]{1,0:T(4,128)S(1)}, s32[3,16384]{1,0:T(4,128)}, u32[]{:S(2)}) copy-start(s32[3,16384]{1,0:T(4,128)} %param.24) | copy-start | bytes 589828
  7.2 80.8 %copy-start.3 = (f32[16384]{0:T(1024)S(1)}, f32[16384]{0:T(1024)}, u32[]{:S(2)}) copy-start(f32[16384]{0:T(1024)} %param.30) | copy-start | bytes 196612
  7.2 79.2 %all-reduce.10.cloned.1.call-start = ((), (), s32[]{:S(2)}) async-start(), calls=%async_computation | async-start | bytes 131072 | tf_op jit(solution)/shard_map/psum | solution.py:110
  14.9 77.1 %copy-start.7 = (s32[1,1,32]{2,1,0:T(1,128)S(1)}, s32[1,1,32]{2,1,0:T(1,128)}, u32[]{:S(2)}) copy-start(s32[1,1,32]{2,1,0:T(1,128)} %param.19) | copy-start | bytes 388
  14.9 78.2 %copy-start = (f32[3,16384]{1,0:T(4,128)S(1)}, f32[3,16384]{1,0:T(4,128)}, u32[]{:S(2)}) copy-start(f32[3,16384]{1,0:T(4,128)} %param.23) | copy-start | bytes 589828
  16.0 186.7 %all-reduce.12.cloned.1.call-start = ((), (), s32[]{:S(2)}) async-start(), calls=%async_computation.1 | async-start | bytes 131072 | tf_op jit(solution)/shard_map/psum | solution.py:116
  93.1 181.0 %all-reduce.14.cloned.1.call-start = ((), (), s32[]{:S(2)}) async-start(), calls=%async_computation.2 | async-start | bytes 131072 | tf_op jit(solution)/shard_map/psum | solution.py:110
  208.8 181.6 %all-reduce.16.cloned.1.call-start = ((), (), s32[]{:S(2)}) async-start(), calls=%async_computation.3 | async-start | bytes 131072 | tf_op jit(solution)/shard_map/psum | solution.py:116
  279.8 183.9 %copy-start.2 = (f32[3,16384]{1,0:T(4,128)S(1)}, f32[3,16384]{1,0:T(4,128)}, u32[]{:S(2)}) copy-start(f32[3,16384]{1,0:T(4,128)} %param.22) | copy-start | bytes 589828
  279.8 183.9 %copy-start.4 = (f32[16384]{0:T(1024)S(1)}, f32[16384]{0:T(1024)}, u32[]{:S(2)}) copy-start(f32[16384]{0:T(1024)} %param.28) | copy-start | bytes 196612
  279.8 183.9 %copy-start.5 = (f32[16384]{0:T(1024)S(1)}, f32[16384]{0:T(1024)}, u32[]{:S(2)}) copy-start(f32[16384]{0:T(1024)} %param.26) | copy-start | bytes 196612
  280.8 182.9 %all-reduce.20.cloned.1.call-start = ((), (), s32[]{:S(2)}) async-start(), calls=%async_computation.5 | async-start | bytes 655360 | tf_op jit(solution)/shard_map/psum | solution.py:110
  396.5 196.9 %all-reduce.18.cloned.1.call-start = ((), (), s32[]{:S(2)}) async-start(), calls=%async_computation.4 | async-start | bytes 655360 | tf_op jit(solution)/shard_map/psum | solution.py:116
Sparse Core Ops, SparseCore 0:
  16.1 70.2 all-reduce.9
  93.3 109.3 all-reduce.11
  208.9 65.1 all-reduce.13
  280.9 109.3 all-reduce.15
  396.6 66.9 all-reduce.19
  478.4 115.0 all-reduce.17
where the time goes:
time: 688 us; the launch traced here: 687 us
  waiting for transfers between devices  527 us (77%)
  blocking collectives  76.4 us (11%)
  matrix products  27.4 us (4%)
  other arithmetic  22.2 us (3%)
  between operations  20.9 us (3%)
  local copies, waits for them, and re-layouts  12.7 us (2%)
    psum x3, waiting for transfers between devices, local(): image_rows = lax.psum(image, 'col')[0]  329 us
    psum x3, waiting for transfers between devices, local(): back = lax.psum(back_partial, 'row')[0]  198 us
    psum x1, blocking collectives, local(): tau_total, sigma_total = lax.psum((tau_local, sigma_local), ('row', 'col'))  76.4 us
    dot_general x8, matrix products, block_terms(): jnp.einsum(einsum_form, tile_part, picked, preferred_element_type=jnp.flo...  24.8 us
  transfers between devices with their start and end apart: 6, of which 6 were waited for; matrix products, arithmetic and copies ran while one was open for 1% of the time, Pallas kernels for 0%

commit v1 on v0

--- a/solution.py
+++ b/solution.py
@@ -107,7 +107,7 @@
         sigma_local = jnp.sum(row_share(dual_term) * residual_share[step])
         spread = dual_term.astype(jnp.bfloat16)
         back_partial = backward(spread[None, :])
-        back = lax.psum(back_partial, "row")[0]
+        back = jnp.sum(lax.all_gather(back_partial, "row"), axis=0)[0]
         primal_term = masks_x[step] * (weight * adjoint_x - 2.0 * sigma * back)
         tau_local = jnp.sum(-column_share(primal_term) * column_share(reduced[step]))
         primal_input = primal_term.astype(jnp.bfloat16)

time: 688 us -> 586 us (0.85)
  waiting for transfers between devices: 527 us -> 363 us
  blocking collectives: 76.4 us -> 142 us
    psum x3 -> x1, waiting for transfers between devices: 198 us -> 36 us  [local(): reduced = cost_vector[None, :] - lax.psum(dual_partial, 'row')]
    all_gather x0 -> x3, blocking collectives: none -> 66.1 us  [local(): back = jnp.sum(lax.all_gather(back_partial, 'row'), axis=0)[0]]
  transfers between devices with their start and end apart: 6 -> 4, of which waited for: 6 -> 4; matrix products, arithmetic and copies ran while one was open for 1% -> 3% of each run, Pallas kernels for 0% -> 0%
where the time goes in v1:
time: 586 us; the launch traced here: 585 us
  waiting for transfers between devices  363 us (62%)
  blocking collectives  142 us (24%)
  matrix products  27.4 us (5%)
  other arithmetic  20.5 us (3%)
  between operations  20.5 us (3%)
  local copies, waits for them, and re-layouts  10.8 us (2%)
    psum x3, waiting for transfers between devices, local(): image_rows = lax.psum(image, 'col')[0]  327 us
    psum x1, blocking collectives, local(): tau_total, sigma_total = lax.psum((tau_local, sigma_local), ('row', 'col'))  76.4 us
    all_gather x3, blocking collectives, local(): back = jnp.sum(lax.all_gather(back_partial, 'row'), axis=0)[0]  66.1 us
    psum x1, waiting for transfers between devices, local(): reduced = cost_vector[None, :] - lax.psum(dual_partial, 'row')  36 us
    dot_general x8, matrix products, block_terms(): jnp.einsum(einsum_form, tile_part, picked, preferred_element_type=jnp.flo...  24.9 us
  transfers between devices with their start and end apart: 4, of which 4 were waited for; matrix products, arithmetic and copies ran while one was open for 3% of the time, Pallas kernels for 0%

profile of v1, /device:TPU:1, one launch (start us, length us, event | category | flops | bytes accessed | tf_op | source)
XLA Modules:
  0.0 585.1 jit_solution(1149535442940587989)
XLA Ops:
  9.9 1.0 convert_element_type.25
  11.1 0.9 fusion.84
  13.4 2.8 fusion.14
  16.6 23.7 %all_gather.9 = f32[8,1,16384]{2,1,0:T(1,128)S(1)} all-gather(f32[1,1,16384]{2,1,0:T(1,128)S(1)} %all_gather_reshape.9), channel_id=1, replica_groups=mesh['row'=8,'col'=32] {'row'}, dimensions={0}, use_global_device_ids=true | all-gather | bytes 589824 | tf_op jit(solution)/shard_map/all_gather | solution.py:110
  42.9 3.4 fusion.12
  48.0 2.9 fusion.19
  50.9 107.9 %all-reduce.7.cloned.1.call-done = f32[1,16384]{1,0:T(1,128)} async-done(((f32[1,16384]{1,0:T(1,128)}), f32[1,16384]{1,0:T(1,128)}) %all-reduce.7.cloned.1.call-update) | async-done | bytes 65552 | tf_op jit(solution)/shard_map/psum | solution.py:116
  158.8 1.5 broadcast_multiply_fusion.2
  161.1 2.8 fusion.10
  164.3 20.9 %all_gather.10 = f32[8,1,16384]{2,1,0:T(1,128)S(1)} all-gather(f32[1,1,16384]{2,1,0:T(1,128)S(1)} %all_gather_reshape.10), channel_id=1, replica_groups=mesh['row'=8,'col'=32] {'row'}, dimensions={0}, use_global_device_ids=true | all-gather | bytes 589824 | tf_op jit(solution)/shard_map/all_gather | solution.py:110
  187.0 3.4 fusion.8
  193.5 107.4 %all-reduce.9.cloned.1.call-done = f32[1,16384]{1,0:T(1,128)} async-done(((f32[1,16384]{1,0:T(1,128)}), f32[1,16384]{1,0:T(1,128)}) %all-reduce.9.cloned.1.call-update) | async-done | bytes 65552 | tf_op jit(solution)/shard_map/psum | solution.py:116
  300.9 1.5 broadcast_multiply_fusion.1
  303.1 2.8 fusion.6
  306.4 21.4 %all_gather.11 = f32[8,1,16384]{2,1,0:T(1,128)S(1)} all-gather(f32[1,1,16384]{2,1,0:T(1,128)S(1)} %all_gather_reshape.11), channel_id=1, replica_groups=mesh['row'=8,'col'=32] {'row'}, dimensions={0}, use_global_device_ids=true | all-gather | bytes 589824 | tf_op jit(solution)/shard_map/all_gather | solution.py:110
  329.5 3.4 fusion.4
  333.9 36.0 %all-reduce.11.cloned.1.call-done = f32[3,16384]{1,0:T(4,128)} async-done(((f32[3,16384]{1,0:T(4,128)}), f32[3,16384]{1,0:T(4,128)}) %all-reduce.11.cloned.1.call-update) | async-done | bytes 196624 | tf_op jit(solution)/shard_map/psum | solution.py:89
  369.9 1.8 subtract_convert_fusion
  372.5 3.4 fusion.25
  380.4 111.8 %all-reduce.13.cloned.1.call-done = (f32[1,16384]{1,0:T(1,128)}, f32[3,16384]{1,0:T(4,128)}) async-done(((f32[1,16384]{1,0:T(1,128)}, f32[3,16384]{1,0:T(4,128)}), (f32[1,16384]{1,0:T(1,128)}, f32[3,16384]{1,0:T(4,128)})) %all-reduce.13.cloned.1.call-update) | async-done | bytes 262160 | tf_op jit(solution)/shard_map/psum | solution.py:116
  493.7 1.5 broadcast_multiply_fusion
  495.2 2.0 multiply_reduce_fusion.3
  499.2 1.2 add_add_fusion
  500.4 76.4 %all-reduce = (f32[]{:T(128)}, f32[]{:T(128)}) all-reduce(f32[]{:T(128)S(6)} %add.114, f32[]{:T(128)S(6)} %add.112), channel_id=1, replica_groups=mesh['row'=8,'col'=32] {'row','col'}, use_global_device_ids=true, to_apply=%region_15.18 | all-reduce | flops 2 | bytes 16 | tf_op jit(solution)/shard_map/psum | solution.py:118
  (93 shorter events, 22.7 us)
Async XLA Ops:
  7.2 9.1 %copy-start.7 = (s32[1,1,32]{2,1,0:T(1,128)S(1)}, s32[1,1,32]{2,1,0:T(1,128)}, u32[]{:S(2)}) copy-start(s32[1,1,32]{2,1,0:T(1,128)} %param.20) | copy-start | bytes 388
  7.2 33.2 %copy-start.6 = (f32[2]{0:T(128)S(1)}, f32[2]{0:T(128)}, u32[]{:S(2)}) copy-start(f32[2]{0:T(128)} %param.29) | copy-start | bytes 28
  7.2 33.8 %copy-start.1 = (s32[3,16384]{1,0:T(4,128)S(1)}, s32[3,16384]{1,0:T(4,128)}, u32[]{:S(2)}) copy-start(s32[3,16384]{1,0:T(4,128)} %param.24) | copy-start | bytes 589828
  7.2 34.9 %copy-start.2 = (f32[16384]{0:T(1024)S(1)}, f32[16384]{0:T(1024)}, u32[]{:S(2)}) copy-start(f32[16384]{0:T(1024)} %param.30) | copy-start | bytes 196612
  7.2 151.6 %all-reduce.7.cloned.1.call-start = ((), (), s32[]{:S(2)}) async-start(), calls=%async_computation | async-start | bytes 131072 | tf_op jit(solution)/shard_map/psum | solution.py:116
  16.2 30.0 %copy-start.8 = (s32[1,1,32]{2,1,0:T(1,128)S(1)}, s32[1,1,32]{2,1,0:T(1,128)}, u32[]{:S(2)}) copy-start(s32[1,1,32]{2,1,0:T(1,128)} %param.19) | copy-start | bytes 388
  16.2 31.1 %copy-start = (f32[3,16384]{1,0:T(4,128)S(1)}, f32[3,16384]{1,0:T(4,128)}, u32[]{:S(2)}) copy-start(f32[3,16384]{1,0:T(4,128)} %param.23) | copy-start | bytes 589828
  47.3 253.6 %all-reduce.9.cloned.1.call-start = ((), (), s32[]{:S(2)}) async-start(), calls=%async_computation.1 | async-start | bytes 131072 | tf_op jit(solution)/shard_map/psum | solution.py:116
  191.4 178.5 %all-reduce.11.cloned.1.call-start = ((), (), s32[]{:S(2)}) async-start(), calls=%async_computation.2 | async-start | bytes 524288 | tf_op jit(solution)/shard_map/psum | solution.py:89
  192.6 299.6 %all-reduce.13.cloned.1.call-start = ((), (), s32[]{:S(2)}) async-start(), calls=%async_computation.3 | async-start | bytes 655360 | tf_op jit(solution)/shard_map/psum | solution.py:116
  306.0 63.9 %copy-start.3 = (f32[3,16384]{1,0:T(4,128)S(1)}, f32[3,16384]{1,0:T(4,128)}, u32[]{:S(2)}) copy-start(f32[3,16384]{1,0:T(4,128)} %param.22) | copy-start | bytes 589828
  306.0 63.9 %copy-start.4 = (f32[16384]{0:T(1024)S(1)}, f32[16384]{0:T(1024)}, u32[]{:S(2)}) copy-start(f32[16384]{0:T(1024)} %param.28) | copy-start | bytes 196612
  306.0 63.9 %copy-start.5 = (f32[16384]{0:T(1024)S(1)}, f32[16384]{0:T(1024)}, u32[]{:S(2)}) copy-start(f32[16384]{0:T(1024)} %param.26) | copy-start | bytes 196612
Sparse Core Ops, SparseCore 0:
  47.4 111.3 all-reduce.6
  191.5 109.3 all-reduce.8
  303.2 66.6 all-reduce.10
  377.2 114.9 all-reduce.12
